TPU v7x, 32 devices: a whole 2x2x4 slice. The times are simulated.
32 devices in a mesh: group: 2 (over y), user: 2 (over core), cand: 8 (over z, x).
Axes of the slice: x: 2, y: 2, z: 4, core: 2. Of those that a mesh axis runs over, the one named last changes fastest.
Arguments:
- history: bfloat16 [4, 1024, 1024], P(('group', 'user'), None, 'cand'), parts along dimension 0, may hold values from -6 to 6
- hist_len: int32 [4], P(('group', 'user')), parts along dimension 0, may hold values from 256 to 1024
- tile_counts: int32 [4, 8], P(('group', 'user'), 'cand'), parts along dimension 0, may hold values from 0 to 3, as said below
- cand_emb: bfloat16 [4, 3072, 1024], P(('group', 'user'), 'cand'), parts along dimension 0, may hold values from -3 to 3
- w_in: bfloat16 [1024, 4096], P(None, 'cand'), may hold values from -1 to 1
- out_gain: float32 [1024], replicated, may hold values from 0.25 to 1.75
- w_out: bfloat16 [1024, 1024], P(None, 'cand'), may hold values from -0.1875 to 0.1875
Outputs:
- cand_out: bfloat16 [4, 3072, 1024], P(('group', 'user'), 'cand'), parts along dimension 0
There are 2 independent parts, one for each index of `group`. A program takes and returns all parts, laid end to end along the dimension named above; an argument that names none is the same for every part. Nothing has to cross between parts.
Inputs may be any that keep to these rules, and one draw needn't show every extreme that they name: In each user's row of tile_counts exactly 1 entries equal 3, 2 * (1) entries are 0 and all others are 1, so that each row sums to its number of entries; which entries take which value is random.
All inputs are finite; a program needn't handle non-finite values.
Results may differ from a plain program's by a relative error of at most 0.0069.
Values may be sent and summed in bfloat16 or wider, within the bound.
A program may use at most 64 MiB of HBM per device.

v0:
```python
import math

import jax
import jax.numpy as jnp
from jax import lax
from jax.sharding import PartitionSpec as P

D = 1024
HEADS = 8
DH = 128
TILE = 128


def layer_norm(values):
    center = values - jnp.mean(values, axis=-1, keepdims=True)
    spread = jnp.mean(center * center, axis=-1, keepdims=True)
    return center * lax.rsqrt(spread + 1e-05)


def attend_rows(carry, kv_piece, queries, length, score_scale):
    key_count = kv_piece.shape[0]
    values = kv_piece[:, :D].reshape(key_count, HEADS, DH)
    key_heads = kv_piece[:, D:].reshape(key_count, HEADS, DH)
    scores = (
        jnp.einsum("rhe,the->hrt", queries, key_heads, preferred_element_type=jnp.float32)
        * score_scale
    )
    positions = jnp.arange(key_count, dtype=jnp.int32)
    weights = jnp.where(positions[None, None, :] < length, jax.nn.silu(scores), 0.0).astype(
        jnp.bfloat16
    )
    mixed_sum = jnp.einsum("hrt,the->rhe", weights, values, preferred_element_type=jnp.float32)
    return mixed_sum.reshape(carry.shape)


def score_rows(embedded, history, length, w_in, out_gain, w_out):
    score_scale = 1.0 / math.sqrt(DH)
    rows_here = embedded.shape[0]
    normed = layer_norm(embedded.astype(jnp.float32)).astype(jnp.bfloat16)
    initial = jnp.zeros((rows_here, D), jnp.float32)
    own_events = lax.all_to_all(history, "cand", split_axis=0, concat_axis=1, tiled=True)
    hist_normed = layer_norm(own_events.astype(jnp.float32)).astype(jnp.bfloat16)
    stacked = jnp.concatenate([normed, hist_normed], axis=0)
    projected = jax.nn.silu(
        jnp.dot(
            stacked,
            lax.all_gather(w_in, "cand", axis=1, tiled=True),
            preferred_element_type=jnp.float32,
        )
    ).astype(jnp.bfloat16)
    proj_rows = projected[:rows_here]
    hist_proj = projected[rows_here:]
    kv_local = jnp.concatenate([hist_proj[:, D : 2 * D], hist_proj[:, 3 * D :]], axis=1)
    queries = proj_rows[:, 2 * D : 3 * D].reshape(rows_here, HEADS, DH)
    summed = attend_rows(
        initial, lax.all_gather(kv_local, "cand", axis=0, tiled=True), queries, length, score_scale
    )
    gate_part = proj_rows[:, :D].astype(jnp.float32)
    cand_values = proj_rows[:, D : 2 * D].reshape(rows_here, HEADS, DH).astype(jnp.float32)
    cand_keys = proj_rows[:, 3 * D :].reshape(rows_here, HEADS, DH).astype(jnp.float32)
    own_score = jax.nn.silu(jnp.sum(queries.astype(jnp.float32) * cand_keys, axis=-1) * score_scale)
    attn = summed + (own_score[:, :, None] * cand_values).reshape(rows_here, D)
    gated = (layer_norm(attn) * out_gain[None, :] * gate_part).astype(jnp.bfloat16)
    residual = embedded.astype(jnp.float32)
    return (
        residual
        + jnp.dot(
            gated,
            lax.all_gather(w_out, "cand", axis=1, tiled=True),
            preferred_element_type=jnp.float32,
        )
    ).astype(jnp.bfloat16)


def shards(history, hist_len, tile_counts, cand_emb, w_in, out_gain, w_out):
    tile_total = tile_counts[0, 0]
    length = hist_len[0]
    slot_rows = cand_emb[0]
    slot_count = slot_rows.shape[0]
    own_history = history[0]
    scored = score_rows(slot_rows, own_history, length, w_in, out_gain, w_out)
    live = jnp.arange(slot_count, dtype=jnp.int32) < tile_total * TILE
    result = jnp.where(live[:, None], scored, jnp.zeros_like(scored))
    return result[None]


def solution(mesh):
    in_specs = (
        P(("group", "user"), None, "cand"),
        P(("group", "user")),
        P(("group", "user"), "cand"),
        P(("group", "user"), "cand", None),
        P(None, "cand"),
        P(),
        P(None, "cand"),
    )
    out_specs = P(("group", "user"), "cand", None)
    return jax.shard_map(shards, mesh=mesh, in_specs=in_specs, out_specs=out_specs, check_vma=False)
```

profile of v0, /device:TPU:0, one launch (start us, length us, event | category | flops | bytes accessed | tf_op | source)
XLA Modules:
  0.0 282.9 jit_solution(6100628635871063216)
XLA Ops:
  6.5 0.0 copy-start
  6.5 0.0 all-gather.4.cloned.1.call-start
  6.5 0.7 all-gather.4.cloned.1.call-update
  7.3 7.3 %all-to-all-start = ((bf16[8,128,128]{2,1,0:T(8,128)(2,1)}), bf16[8,128,128]{2,1,0:T(8,128)(2,1)S(1)}, u32[]{:S(2)}, u32[]{:S(2)}) async-start(bf16[8,128,128]{2,1,0:T(8,128)(2,1)} %bitcast.72), calls=%async_computation | async-start | bytes 524288 | tf_op jit(solution)/shard_map/all_to_all | solution.py:41
  14.5 0.0 all-gather.6.cloned.1.call-start
  14.6 0.0 copy-done
  14.6 0.2 convert_reduce_fusion
  14.8 0.3 fusion.11
  15.1 0.3 fusion.12
  15.4 8.1 %all-to-all-done = bf16[8,128,128]{2,1,0:T(8,128)(2,1)S(1)} async-done(((bf16[8,128,128]{2,1,0:T(8,128)(2,1)}), bf16[8,128,128]{2,1,0:T(8,128)(2,1)S(1)}, u32[]{:S(2)}, u32[]{:S(2)}) %all-to-all-start) | async-done | bytes 262176 | tf_op jit(solution)/shard_map/all_to_all | solution.py:41
  23.5 0.1 convert_reduce_fusion.1
  23.6 0.2 fusion.32
  23.8 0.2 fusion.34
  24.1 113.9 %all-gather.4.cloned.1.call-done = bf16[1024,4096]{1,0:T(8,128)(2,1)} async-done(((bf16[1024,512]{1,0:T(8,128)(2,1)}), bf16[1024,4096]{1,0:T(8,128)(2,1)}) %all-gather.4.cloned.1.call-update) | async-done | bytes 8388624 | tf_op jit(solution)/shard_map/all_gather | solution.py:47
  137.9 8.6 %multiply_convert_fusion = bf16[512,4096]{1,0:T(8,128)(2,1)S(1)} fusion(bf16[1024,4096]{1,0:T(8,128)(2,1)} %all-gather.4.cloned.1.call-done, bf16[128,1024]{1,0:T(8,128)(2,1)S(1)} %fusion.34, bf16[384,1024]{1,0:T(8,128)(2,1)S(1)} %fusion.12), kind=kOutput, calls=%fused_computation.1 | convolution fusion | flops 4307550208 | bytes 13631488 | tf_op jit(solution)/shard_map/dot_general | solution.py:45
  146.6 0.0 copy-start.2
  146.6 1.9 copy-done.2
  148.5 0.9 pad_maximum_fusion
  149.4 0.0 all-gather.6.cloned.1.call-update
  149.4 0.0 all-gather.8.cloned.1.call-start
  149.5 0.7 all-gather.8.cloned.1.call-update
  151.5 2.6 slice_bitcast_fusion.2
  154.1 0.3 copy.37
  154.4 0.2 copy.36
  154.6 0.5 multiply_reduce_fusion.1
  155.1 0.1 copy.29
  155.2 0.1 copy.30
  155.3 65.8 %all-gather.6.cloned.1.call-done = bf16[1024,2048]{1,0:T(8,128)(2,1)} async-done(((bf16[128,2048]{1,0:T(8,128)(2,1)}), bf16[1024,2048]{1,0:T(8,128)(2,1)}) %all-gather.6.cloned.1.call-update) | async-done | bytes 4194320 | tf_op jit(solution)/shard_map/all_gather | solution.py:56
  221.2 4.2 %slice_bitcast_fusion = (bf16[128,8,8,128]{3,2,1,0:T(8,128)(2,1)}, bf16[1024,1024]{1,0:T(8,128)(2,1)S(1)}) fusion(bf16[1024,2048]{1,0:T(8,128)(2,1)} %all-gather.6.cloned.1.call-done), kind=kLoop, calls=%fused_computation.6 | loop fusion | bytes 8388608
  225.4 2.6 copy.31
  227.9 7.5 %fusion = f32[8,128,384]{2,1,0:T(8,128)S(1)} fusion(bf16[1024,8,128]{0,2,1:T(8,128)(2,1)} %bitcast.70, pred[1024]{0:T(1024)(128)(4,1)S(1)} %iota_compare_fusion, bf16[128,8,8,128]{3,2,1,0:T(8,128)(2,1)} %get-tuple-element.10, bf16[48,8,8,128]{3,2,1,0:T(8,128)(2,1)} %get-tuple-element.8), kind=kOutput, calls=%fused_computation.2 | convolution fusion | flops 1632632832 | bytes 6554624 | tf_op jit(solution)/shard_map/hrt,the->rhe/dot_general | solution.py:32
  235.4 1.6 copy.32
  237.1 0.0 copy-start.1
  237.1 0.5 mul.114
  237.6 0.9 copy-done.1
  238.5 0.0 copy-start.3
  238.5 1.7 fusion.39
  240.2 0.3 multiply_reduce_fusion
  240.5 32.1 %all-gather.8.cloned.1.call-done = bf16[1024,1024]{1,0:T(8,128)(2,1)} async-done(((bf16[1024,128]{1,0:T(8,128)(2,1)}), bf16[1024,1024]{1,0:T(8,128)(2,1)}) %all-gather.8.cloned.1.call-update) | async-done | bytes 2097168 | tf_op jit(solution)/shard_map/all_gather | solution.py:69
  272.6 0.0 copy-done.3
  272.6 3.8 %fusion.16 = bf16[1,384,1024]{2,1,0:T(8,128)(2,1)} fusion(bf16[1024,1024]{1,0:T(8,128)(2,1)} %all-gather.8.cloned.1.call-done, bf16[1,384,1024]{2,1,0:T(8,128)(2,1)S(1)} %copy-done, f32[384,1024]{1,0:T(8,128)S(1)} %get-tuple-element.6, bf16[512,4096]{1,0:T(8,128)(2,1)} %copy-done.2, f32[1024]{0:T(1024)S(1)} %copy-done.3, f32[384]{0:T(512)S(1)} %add_rsqrt_fusion, ...), kind=kOutput, calls=%fused_computation.23 | convolution fusion | flops 809238528 | bytes 6036864 | tf_op jit(solution)/shard_map/dot_general | solution.py:67
  (10 shorter events, 0.1 us)
Async XLA Ops:
  6.5 8.0 %copy-start = (bf16[1,384,1024]{2,1,0:T(8,128)(2,1)S(1)}, bf16[1,384,1024]{2,1,0:T(8,128)(2,1)}, u32[]{:S(2)}) copy-start(bf16[1,384,1024]{2,1,0:T(8,128)(2,1)} %param.10) | copy-start | bytes 2359300
  6.5 131.4 %all-gather.4.cloned.1.call-start = ((), (), s32[]{:S(2)}) async-start(), calls=%async_computation.1 | async-start | bytes 9437184 | tf_op jit(solution)/shard_map/all_gather | solution.py:47
  7.3 16.2 %all-to-all-start = ((bf16[8,128,128]{2,1,0:T(8,128)(2,1)}), bf16[8,128,128]{2,1,0:T(8,128)(2,1)S(1)}, u32[]{:S(2)}, u32[]{:S(2)}) async-start(bf16[8,128,128]{2,1,0:T(8,128)(2,1)} %bitcast.72), calls=%async_computation | async-start | bytes 524288 | tf_op jit(solution)/shard_map/all_to_all | solution.py:41
  14.5 206.6 %all-gather.6.cloned.1.call-start = ((), (), s32[]{:S(2)}) async-start(), calls=%async_computation.2 | async-start | bytes 4718592 | tf_op jit(solution)/shard_map/all_gather | solution.py:56
  146.6 1.9 copy-start.2
  149.4 123.2 %all-gather.8.cloned.1.call-start = ((), (), s32[]{:S(2)}) async-start(), calls=%async_computation.3 | async-start | bytes 2359296 | tf_op jit(solution)/shard_map/all_gather | solution.py:69
  237.1 1.4 copy-start.1
  238.5 34.1 %copy-start.3 = (f32[1024]{0:T(1024)S(1)}, f32[1024]{0:T(1024)}, u32[]{:S(2)}) copy-start(f32[1024]{0:T(1024)} %param.12) | copy-start | bytes 12292
Sparse Core Ops, SparseCore 0:
  9.4 128.4 all-gather.3
  149.5 71.5 all-gather.5
  223.2 49.3 all-gather.7
where the time goes:
time: 283 us
  waiting for transfers between devices  221 us (78%)
  matrix products  19.9 us (7%)
  between operations  14.5 us (5%)
  local copies, waits for them, and re-layouts  12.5 us (4%)
  other arithmetic  7.38 us (3%)
  starting transfers between devices  7.35 us (3%)
    all_gather x1, waiting for transfers between devices, score_rows(): lax.all_gather(w_in, 'cand', axis=1, tiled=True)  114 us
    all_gather x1, waiting for transfers between devices, score_rows(): lax.all_gather(kv_local, 'cand', axis=0, tiled=True)  65.8 us
    all_gather x1, waiting for transfers between devices, score_rows(): lax.all_gather(w_out, 'cand', axis=1, tiled=True)  32.1 us
    dot_general x1, matrix products, score_rows(): jnp.dot(stacked, lax.all_gather(w_in, 'cand', axis=1, tiled=True), prefer...  8.61 us
    all_to_all x1, waiting for transfers between devices, score_rows(): lax.all_to_all(history, 'cand', split_axis=0, concat_axis=1, tiled=True)  8.08 us
    unnamed x11, local copies, waits for them, and re-layouts  7.59 us
    dot_general x1, matrix products, attend_rows(): jnp.einsum('hrt,the->rhe', weights, values, preferred_element_type=jnp.fl...  7.51 us
    all_to_all x1, starting transfers between devices, score_rows(): lax.all_to_all(history, 'cand', split_axis=0, concat_axis=1, tiled=True)  7.26 us
  transfers between devices with their start and end apart: 4, of which 4 were waited for; matrix products, arithmetic and copies ran while one was open for 8% of the time, Pallas kernels for 0%

commit v1 on v0

--- a/solution.py
+++ b/solution.py
@@ -1,20 +1,316 @@
+import functools
 import math
 
 import jax
 import jax.numpy as jnp
 from jax import lax
+from jax.experimental import pallas as pl
+from jax.experimental.pallas import tpu as pltpu
 from jax.sharding import PartitionSpec as P
 
 D = 1024
 HEADS = 8
 DH = 128
 TILE = 128
+RING = 8
+MESH = pl.DeviceIdType.MESH
 
 
 def layer_norm(values):
     center = values - jnp.mean(values, axis=-1, keepdims=True)
     spread = jnp.mean(center * center, axis=-1, keepdims=True)
     return center * lax.rsqrt(spread + 1e-05)
+
+
+def half_silu(half):
+    return half + half * jnp.tanh(half)
+
+
+def cand_of(place):
+    high = place // 4
+    return (1 - high) * (2 * place) + high * (15 - 2 * place)
+
+
+def place_of(cand):
+    row, column = cand // 2, cand % 2
+    return (1 - column) * row + column * (7 - row)
+
+
+def fused_kernel(
+    length_ref, count_ref, hist_ref, w_ref, wo_ref, cand_ref, gain_ref, out_ref,
+    hb, wb, ob, nb, hn, pb, kvb, ab, gb,
+    ring_send, ring_recv, side_send, side_recv, local_sem,
+):
+    group = lax.axis_index("group")
+    user = lax.axis_index("user")
+    me = lax.axis_index("cand")
+    place = place_of(me)
+    slots = cand_ref.shape[1]
+    events = hist_ref.shape[1]
+
+    def shard_at(offset):
+        return cand_of((place + offset + RING) % RING)
+
+    core_peer = {"user": 1 - user}
+    y_peer = {"group": 1 - group}
+    ring_peer = ({"cand": shard_at(1)}, {"cand": shard_at(-1)})
+    started = []
+
+    quarter = D // 4
+    half = D // 2
+    w_start = (2 * group + user) * quarter
+    w_core = (2 * group + 1 - user) * quarter
+    w_y = (2 * (1 - group) + user) * quarter
+    w_diag = (2 * (1 - group) + 1 - user) * quarter
+    o_start = user * half
+    o_core = (1 - user) * half
+    kinds = (
+        (w_ref, wb, w_start, quarter),
+        (hist_ref.at[0], hb, 0, events),
+        (wo_ref, ob, o_start, half),
+    )
+
+    barrier = pltpu.get_barrier_semaphore()
+    for peer in (ring_peer[0], ring_peer[1], core_peer, y_peer):
+        pl.semaphore_signal(barrier, inc=1, device_id=peer, device_id_type=MESH)
+    pl.semaphore_wait(barrier, 4)
+
+    def ring_copy(kind, way, step, shard, first):
+        source, buffer, start, size = kinds[kind]
+        if step == 3:
+            size = size // 2
+            start = start + way * size
+        rows = pl.ds(pl.multiple_of(start, 64), size)
+        spot = buffer.at[shard, rows, :]
+        return pltpu.make_async_remote_copy(
+            src_ref=source.at[rows, :] if first else spot,
+            dst_ref=spot,
+            send_sem=ring_send.at[kind, way, step],
+            recv_sem=ring_recv.at[kind, way, step],
+            device_id=ring_peer[way],
+            device_id_type=MESH,
+        )
+
+    def ring_start(kind, step):
+        for way in range(2):
+            shard = shard_at(-step if way == 0 else step)
+            copy = ring_copy(kind, way, step, shard, step == 0)
+            copy.start()
+            started.append(copy)
+
+    def ring_wait(kind, step):
+        for way in range(2):
+            shard = shard_at(-1 - step if way == 0 else step + 1)
+            ring_copy(kind, way, step, shard, False).wait_recv()
+
+    def spots(step):
+        return ((6, 4),) if step == 3 else ((2 * step, -1 - step), (2 * step + 1, step + 1))
+
+    def side_copy(kind, index, offset):
+        buffer, start, size, peer = (
+            (wb, w_start, quarter, core_peer),
+            (wb, w_start, quarter, y_peer),
+            (wb, w_y, quarter, core_peer),
+            (ob, o_start, half, core_peer),
+        )[kind]
+        spot = buffer.at[shard_at(offset), pl.ds(pl.multiple_of(start, 256), size), :]
+        return pltpu.make_async_remote_copy(
+            src_ref=spot, dst_ref=spot,
+            send_sem=side_send.at[kind, index], recv_sem=side_recv.at[kind, index],
+            device_id=peer, device_id_type=MESH,
+        )
+
+    def side_start(kind, step):
+        for index, offset in spots(step):
+            copy = side_copy(kind, index, offset)
+            copy.start()
+            started.append(copy)
+
+    def side_wait(kind, step):
+        for index, offset in spots(step):
+            buffer, start, size, peer = (
+                (wb, w_core, quarter, core_peer),
+                (wb, w_y, quarter, y_peer),
+                (wb, w_diag, quarter, core_peer),
+                (ob, o_core, half, core_peer),
+            )[kind]
+            spot = buffer.at[shard_at(offset), pl.ds(pl.multiple_of(start, 256), size), :]
+            pltpu.make_async_remote_copy(
+                src_ref=spot, dst_ref=spot,
+                send_sem=side_send.at[kind, index], recv_sem=side_recv.at[kind, index],
+                device_id=peer, device_id_type=MESH,
+            ).wait_recv()
+
+    W, H, O = 0, 1, 2
+    CORE, Y, DIAG, OCORE = 0, 1, 2, 3
+
+    ring_start(W, 0)
+    ring_start(H, 0)
+    own = [
+        pltpu.make_async_copy(w_ref, wb.at[me], local_sem.at[0]),
+        pltpu.make_async_copy(hist_ref.at[0], hb.at[me], local_sem.at[1]),
+        pltpu.make_async_copy(wo_ref, ob.at[me], local_sem.at[2]),
+    ]
+    for copy in own:
+        copy.start()
+    nb[...] = layer_norm(cand_ref[0].astype(jnp.float32)).astype(jnp.bfloat16)
+    for copy in own:
+        copy.wait()
+
+    def project_cand(shard):
+        product = jnp.dot(nb[...], wb[shard], preferred_element_type=jnp.float32)
+        act = half_silu(0.5 * product).astype(jnp.bfloat16)
+        for i in range(4):
+            pb[4 * shard + i] = act[:, i * DH : (i + 1) * DH]
+
+    def project_pair(step):
+        @pl.loop(0, 2)
+        def _(way):
+            project_cand(shard_at((1 - 2 * way) * (step + 1)))
+
+    project_cand(me)
+    for step in range(4):
+        ring_wait(W, step)
+        if step < 3:
+            ring_start(W, step + 1)
+        side_start(Y, step)
+        side_start(CORE, step)
+        ring_wait(H, step)
+        if step < 3:
+            ring_start(H, step + 1)
+        if step >= 1:
+            ring_wait(O, step - 1)
+        ring_start(O, step)
+        if step >= 1:
+            side_start(OCORE, step - 1)
+            side_wait(Y, step - 1)
+            side_start(DIAG, step - 1)
+            side_wait(CORE, step - 1)
+            side_wait(DIAG, step - 1)
+            if step < 3:
+                project_pair(step - 1)
+
+    chunk = 128
+
+    @pl.loop(0, events // chunk)
+    def _(i):
+        rows = pl.ds(pl.multiple_of(i * chunk, chunk), chunk)
+        whole = jnp.concatenate([hb[c, rows, :] for c in range(RING)], axis=1)
+        hn[rows, :] = layer_norm(whole.astype(jnp.float32)).astype(jnp.bfloat16)
+
+    length = length_ref[0]
+    block = 256
+
+    def project_hist(shard):
+        @pl.when((shard % 4) // 2 == 1)
+        def _():
+            first = 4 * shard - 8 - 8 * (shard // 4)
+
+            @pl.loop(0, events // block)
+            def _(i):
+                start = pl.multiple_of(i * block, block)
+                rows = pl.ds(start, block)
+                product = jnp.dot(hn[rows, :], wb[shard], preferred_element_type=jnp.float32)
+                act = half_silu(0.5 * product)
+                event = lax.broadcasted_iota(jnp.int32, act.shape, 0) + start
+                act = jnp.where(event < length, act, 0.0).astype(jnp.bfloat16)
+                for j in range(4):
+                    kvb[first + j, rows, :] = act[:, j * DH : (j + 1) * DH]
+
+    @pl.loop(-2, 3)
+    def _(offset):
+        project_hist(shard_at(offset))
+
+    project_pair(2)
+    project_hist(shard_at(3))
+    project_hist(shard_at(-3))
+    ring_wait(O, 3)
+    side_start(OCORE, 3)
+    side_wait(Y, 3)
+    side_start(DIAG, 3)
+    side_wait(CORE, 3)
+    side_wait(DIAG, 3)
+    project_cand(shard_at(4))
+    project_hist(shard_at(4))
+
+    half_scale = 0.5 / math.sqrt(DH)
+
+    @pl.loop(0, HEADS)
+    def _(head):
+        query = pb[2 * HEADS + head]
+        scores = lax.dot_general(
+            query, kvb[HEADS + head], (((1,), (1,)), ((), ())),
+            preferred_element_type=jnp.float32,
+        )
+        weights = half_silu(scores * half_scale).astype(jnp.bfloat16)
+        mixed = jnp.dot(weights, kvb[head], preferred_element_type=jnp.float32)
+        own_sum = jnp.sum(
+            query.astype(jnp.float32) * pb[3 * HEADS + head].astype(jnp.float32),
+            axis=-1, keepdims=True,
+        )
+        own_weight = half_silu(own_sum * half_scale)
+        ab[head] = mixed + own_weight * pb[HEADS + head].astype(jnp.float32)
+
+    for step in range(4):
+        side_wait(OCORE, step)
+
+    count = count_ref[0, 0]
+
+    @pl.loop(0, slots // chunk)
+    def _(i):
+        start = pl.multiple_of(i * chunk, chunk)
+        rows = pl.ds(start, chunk)
+        attn = jnp.concatenate([ab[h, rows, :] for h in range(HEADS)], axis=1)
+        gate = jnp.concatenate([pb[h, rows, :] for h in range(HEADS)], axis=1)
+        gb[rows, :] = (layer_norm(attn) * gain_ref[...] * gate.astype(jnp.float32)).astype(
+            jnp.bfloat16
+        )
+
+    for j in range(4):
+        columns = pl.ds(j * 256, 256)
+        pair = jnp.concatenate([ob[2 * j], ob[2 * j + 1]], axis=1)
+        added = jnp.dot(gb[...], pair, preferred_element_type=jnp.float32)
+        result = cand_ref[0, :, columns].astype(jnp.float32) + added
+        slot = lax.broadcasted_iota(jnp.int32, result.shape, 0)
+        out_ref[0, :, columns] = jnp.where(slot < count * TILE, result, 0.0).astype(jnp.bfloat16)
+
+    for copy in started:
+        copy.wait_send()
+
+
+def fused_shards(history, hist_len, tile_counts, cand_emb, w_in, out_gain, w_out):
+    slots = cand_emb.shape[1]
+    events = history.shape[1]
+    blocks = 4 * D // DH
+    anywhere = pl.BlockSpec(memory_space=pl.ANY)
+    vmem = pl.BlockSpec(memory_space=pltpu.VMEM)
+    smem = pl.BlockSpec(memory_space=pltpu.SMEM)
+    return pl.pallas_call(
+        fused_kernel,
+        out_shape=jax.ShapeDtypeStruct(cand_emb.shape, jnp.bfloat16),
+        in_specs=[smem, smem, anywhere, anywhere, anywhere, vmem, vmem],
+        out_specs=vmem,
+        scratch_shapes=[
+            pltpu.VMEM((RING, events, D // RING), jnp.bfloat16),
+            pltpu.VMEM((RING, D, 4 * D // RING), jnp.bfloat16),
+            pltpu.VMEM((RING, D, D // RING), jnp.bfloat16),
+            pltpu.VMEM((slots, D), jnp.bfloat16),
+            pltpu.VMEM((events, D), jnp.bfloat16),
+            pltpu.VMEM((blocks, slots, DH), jnp.bfloat16),
+            pltpu.VMEM((blocks // 2, events, DH), jnp.bfloat16),
+            pltpu.VMEM((HEADS, slots, DH), jnp.float32),
+            pltpu.VMEM((slots, D), jnp.bfloat16),
+            pltpu.SemaphoreType.DMA((3, 2, 4)),
+            pltpu.SemaphoreType.DMA((3, 2, 4)),
+            pltpu.SemaphoreType.DMA((4, 7)),
+            pltpu.SemaphoreType.DMA((4, 7)),
+            pltpu.SemaphoreType.DMA((3,)),
+        ],
+        compiler_params=pltpu.CompilerParams(
+            collective_id=0, has_side_effects=True, vmem_limit_bytes=56 * 1024 * 1024
+        ),
+        name="score_fused",
+    )(hist_len, tile_counts, history, w_in, w_out, cand_emb, out_gain.reshape(1, D))
 
 
 def attend_rows(carry, kv_piece, queries, length, score_scale):
@@ -95,4 +391,6 @@
         P(None, "cand"),
     )
     out_specs = P(("group", "user"), "cand", None)
-    return jax.shard_map(shards, mesh=mesh, in_specs=in_specs, out_specs=out_specs, check_vma=False)
+    sizes = tuple(mesh.shape[name] for name in ("group", "user", "cand"))
+    body = fused_shards if sizes == (2, 2, RING) else shards
+    return jax.shard_map(body, mesh=mesh, in_specs=in_specs, out_specs=out_specs, check_vma=False)

time: 283 us -> 82.4 us (0.29)
  waiting for transfers between devices: 221 us -> 0 us
  Pallas kernels: 0 us -> 78.8 us
  matrix products: 19.9 us -> 0 us
  between operations: 14.5 us -> 1.3 us
  local copies, waits for them, and re-layouts: 12.5 us -> 2.06 us
  other arithmetic: 7.38 us -> 0 us
  starting transfers between devices: 7.35 us -> 0 us
    all_gather x3 -> x0, waiting for transfers between devices: 212 us -> none  [the longest x1 114 us: score_rows(): lax.all_gather(w_in, 'cand', axis=1, tiled=True)]
    pallas_call x0 -> x1, Pallas kernels: none -> 78.8 us  [fused_shards(): pl.pallas_call(fused_kernel, out_shape=jax.ShapeDtypeStruct(cand_emb.shap...]
    dot_general x3 -> x0, matrix products: 19.9 us -> none  [the longest x1 8.61 us: score_rows(): jnp.dot(stacked, lax.all_gather(w_in, 'cand', axis=1, tiled=True), prefer...]
    all_to_all x1 -> x0, waiting for transfers between devices: 8.08 us -> none  [score_rows(): lax.all_to_all(history, 'cand', split_axis=0, concat_axis=1, tiled=True)]
    all_to_all x1 -> x0, starting transfers between devices: 7.26 us -> none  [score_rows(): lax.all_to_all(history, 'cand', split_axis=0, concat_axis=1, tiled=True)]
    unnamed x11 -> x1, local copies, waits for them, and re-layouts: 7.59 us -> 2.06 us
    reshape x2 -> x0, local copies, waits for them, and re-layouts: 4.2 us -> none  [the longest x1 2.56 us: attend_rows(): values = kv_piece[:, :D].reshape(key_count, HEADS, DH)]
    reduce_sum x7 -> x0, other arithmetic: 3.32 us -> none  [the longest x3 1.96 us: layer_norm(): center = values - jnp.mean(values, axis=-1, keepdims=True)]
  transfers between devices with their start and end apart: 4 -> 0, of which waited for: 4 -> 0; matrix products, arithmetic and copies ran while one was open for 8% -> 0% of each run, Pallas kernels for 0% -> 0%
where the time goes in v1:
time: 82.4 us; the launch traced here: 82.2 us
  Pallas kernels  78.8 us (96%)
  local copies, waits for them, and re-layouts  2.06 us (2%)
  between operations  1.3 us (2%)
    pallas_call x1, Pallas kernels, fused_shards(): pl.pallas_call(fused_kernel, out_shape=jax.ShapeDtypeStruct(cand_emb.shap...  78.8 us
    unnamed x1, local copies, waits for them, and re-layouts  2.06 us

profile of v1, /device:TPU:0, one launch (start us, length us, event | category | flops | bytes accessed | tf_op | source)
XLA Modules:
  0.0 82.2 jit_solution(5887738005693410560)
XLA Ops:
  1.3 78.8 %score_fused.1 = bf16[1,384,1024]{2,1,0:T(8,128)(2,1)} custom-call(s32[1]{0:T(128)S(6)} %copy.9.length_ref, s32[1,1]{1,0:T(1,128)S(6)} %copy.10.count_ref, bf16[1,1024,128]{2,1,0:T(8,128)(2,1)} %hist_ref.1, bf16[1024,512]{1,0:T(8,128)(2,1)} %w_ref.1, bf16[1024,128]{1,0:T(8,128)(2,1)} %wo_ref.1, bf16[1,384,1024]{2,1,0:T(8,128)(2,1)} %cand_ref.1, ...), custom_call_target="tpu_custom_call" | custom-call | tf_op jit(solution)/shard_map/score_fused/pallas_call | solution.py:288
  80.1 2.1 %copy.11 = bf16[1,384,1024]{2,1,0:T(8,128)(2,1)} copy(bf16[1,384,1024]{2,1,0:T(8,128)(2,1)} %score_fused.1) | data formatting | bytes 1572864

commit v2 on v1

--- a/solution.py
+++ b/solution.py
@@ -37,7 +37,7 @@
 
 
 def fused_kernel(
-    length_ref, count_ref, hist_ref, w_ref, wo_ref, cand_ref, gain_ref, out_ref,
+    length_ref, hist_ref, w_ref, wo_ref, cand_ref, gain_ref, out_ref,
     hb, wb, ob, nb, hn, pb, kvb, ab, gb,
     ring_send, ring_recv, side_send, side_recv, local_sem,
 ):
@@ -168,8 +168,7 @@
         def _(way):
             project_cand(shard_at((1 - 2 * way) * (step + 1)))
 
-    project_cand(me)
-    for step in range(4):
+    def spread_rows(step):
         ring_wait(W, step)
         if step < 3:
             ring_start(W, step + 1)
@@ -178,28 +177,22 @@
         ring_wait(H, step)
         if step < 3:
             ring_start(H, step + 1)
-        if step >= 1:
-            ring_wait(O, step - 1)
-        ring_start(O, step)
-        if step >= 1:
-            side_start(OCORE, step - 1)
-            side_wait(Y, step - 1)
-            side_start(DIAG, step - 1)
-            side_wait(CORE, step - 1)
-            side_wait(DIAG, step - 1)
-            if step < 3:
-                project_pair(step - 1)
+
+    def spread_out(step):
+        ring_wait(O, step)
+        if step < 3:
+            ring_start(O, step + 1)
+        side_start(OCORE, step)
+
+    def gather_rows(step):
+        side_wait(Y, step)
+        side_start(DIAG, step)
+        side_wait(CORE, step)
+        side_wait(DIAG, step)
 
     chunk = 128
-
-    @pl.loop(0, events // chunk)
-    def _(i):
-        rows = pl.ds(pl.multiple_of(i * chunk, chunk), chunk)
-        whole = jnp.concatenate([hb[c, rows, :] for c in range(RING)], axis=1)
-        hn[rows, :] = layer_norm(whole.astype(jnp.float32)).astype(jnp.bfloat16)
-
+    block = 512
     length = length_ref[0]
-    block = 256
 
     def project_hist(shard):
         @pl.when((shard % 4) // 2 == 1)
@@ -217,44 +210,75 @@
                 for j in range(4):
                     kvb[first + j, rows, :] = act[:, j * DH : (j + 1) * DH]
 
-    @pl.loop(-2, 3)
+    half_scale = 0.5 / math.sqrt(DH)
+
+    def attend(first):
+        @pl.loop(0, HEADS // 2)
+        def _(i):
+            head = first + i
+            query = pb[2 * HEADS + head]
+            scores = lax.dot_general(
+                query, kvb[HEADS + head], (((1,), (1,)), ((), ())),
+                preferred_element_type=jnp.float32,
+            )
+            weights = half_silu(scores * half_scale).astype(jnp.bfloat16)
+            mixed = jnp.dot(weights, kvb[head], preferred_element_type=jnp.float32)
+            own_sum = jnp.sum(
+                query.astype(jnp.float32) * pb[3 * HEADS + head].astype(jnp.float32),
+                axis=-1, keepdims=True,
+            )
+            own_weight = half_silu(own_sum * half_scale)
+            ab[head] = mixed + own_weight * pb[HEADS + head].astype(jnp.float32)
+
+    project_cand(me)
+    spread_rows(0)
+    spread_rows(1)
+    ring_start(O, 0)
+    gather_rows(0)
+    project_pair(0)
+    spread_rows(2)
+    spread_out(0)
+    gather_rows(1)
+    project_pair(1)
+    spread_rows(3)
+    spread_out(1)
+    @pl.loop(0, events // chunk)
+    def _(i):
+        rows = pl.ds(pl.multiple_of(i * chunk, chunk), chunk)
+        whole = jnp.concatenate([hb[c, rows, :] for c in range(RING)], axis=1)
+        hn[rows, :] = layer_norm(whole.astype(jnp.float32)).astype(jnp.bfloat16)
+
+    gather_rows(2)
+
+    @pl.loop(-1, 2)
     def _(offset):
         project_hist(shard_at(offset))
 
+    spread_out(2)
+
+    @pl.loop(0, 2)
+    def _(i):
+        project_hist(shard_at(2 - 4 * i))
+
     project_pair(2)
-    project_hist(shard_at(3))
-    project_hist(shard_at(-3))
-    ring_wait(O, 3)
-    side_start(OCORE, 3)
+    spread_out(3)
     side_wait(Y, 3)
     side_start(DIAG, 3)
+
+    @pl.loop(0, 2)
+    def _(i):
+        project_hist(shard_at(3 - 6 * i))
+
+    near = (HEADS // 2) * (me % 2)
+    attend(near)
     side_wait(CORE, 3)
     side_wait(DIAG, 3)
     project_cand(shard_at(4))
     project_hist(shard_at(4))
-
-    half_scale = 0.5 / math.sqrt(DH)
-
-    @pl.loop(0, HEADS)
-    def _(head):
-        query = pb[2 * HEADS + head]
-        scores = lax.dot_general(
-            query, kvb[HEADS + head], (((1,), (1,)), ((), ())),
-            preferred_element_type=jnp.float32,
-        )
-        weights = half_silu(scores * half_scale).astype(jnp.bfloat16)
-        mixed = jnp.dot(weights, kvb[head], preferred_element_type=jnp.float32)
-        own_sum = jnp.sum(
-            query.astype(jnp.float32) * pb[3 * HEADS + head].astype(jnp.float32),
-            axis=-1, keepdims=True,
-        )
-        own_weight = half_silu(own_sum * half_scale)
-        ab[head] = mixed + own_weight * pb[HEADS + head].astype(jnp.float32)
+    attend(HEADS // 2 - near)
 
     for step in range(4):
         side_wait(OCORE, step)
-
-    count = count_ref[0, 0]
 
     @pl.loop(0, slots // chunk)
     def _(i):
@@ -271,8 +295,7 @@
         pair = jnp.concatenate([ob[2 * j], ob[2 * j + 1]], axis=1)
         added = jnp.dot(gb[...], pair, preferred_element_type=jnp.float32)
         result = cand_ref[0, :, columns].astype(jnp.float32) + added
-        slot = lax.broadcasted_iota(jnp.int32, result.shape, 0)
-        out_ref[0, :, columns] = jnp.where(slot < count * TILE, result, 0.0).astype(jnp.bfloat16)
+        out_ref[0, :, columns] = result.astype(jnp.bfloat16)
 
     for copy in started:
         copy.wait_send()
@@ -285,10 +308,10 @@
     anywhere = pl.BlockSpec(memory_space=pl.ANY)
     vmem = pl.BlockSpec(memory_space=pltpu.VMEM)
     smem = pl.BlockSpec(memory_space=pltpu.SMEM)
-    return pl.pallas_call(
+    scored = pl.pallas_call(
         fused_kernel,
         out_shape=jax.ShapeDtypeStruct(cand_emb.shape, jnp.bfloat16),
-        in_specs=[smem, smem, anywhere, anywhere, anywhere, vmem, vmem],
+        in_specs=[smem, anywhere, anywhere, anywhere, vmem, vmem],
         out_specs=vmem,
         scratch_shapes=[
             pltpu.VMEM((RING, events, D // RING), jnp.bfloat16),
@@ -310,7 +333,9 @@
             collective_id=0, has_side_effects=True, vmem_limit_bytes=56 * 1024 * 1024
         ),
         name="score_fused",
-    )(hist_len, tile_counts, history, w_in, w_out, cand_emb, out_gain.reshape(1, D))
+    )(hist_len, history, w_in, w_out, cand_emb, out_gain.reshape(1, D))
+    live = jnp.arange(slots, dtype=jnp.int32) < tile_counts[0, 0] * TILE
+    return jnp.where(live[None, :, None], scored, jnp.zeros_like(scored))
 
 
 def attend_rows(carry, kv_piece, queries, length, score_scale):

time: 82.4 us -> 77 us (0.934)
  Pallas kernels: 78.8 us -> 73.2 us
  other arithmetic: 0 us -> 2.15 us
  local copies, waits for them, and re-layouts: 2.06 us -> 0 us
    pallas_call x1, Pallas kernels: 78.8 us -> 73.2 us  [fused_shards(): pl.pallas_call(fused_kernel, out_shape=jax.ShapeDtypeStruct(cand_emb.shap...]
    select_n x0 -> x1, other arithmetic: none -> 2.14 us  [fused_shards(): return jnp.where(live[None, :, None], scored, jnp.zeros_like(scored))]
    unnamed x1 -> x0, local copies, waits for them, and re-layouts: 2.06 us -> none
where the time goes in v2:
time: 77 us; the launch traced here: 76.7 us
  Pallas kernels  73.2 us (95%)
  other arithmetic  2.15 us (3%)
  between operations  1.31 us (2%)
    pallas_call x1, Pallas kernels, fused_shards(): pl.pallas_call(fused_kernel, out_shape=jax.ShapeDtypeStruct(cand_emb.shap...  73.2 us
    select_n x1, other arithmetic, fused_shards(): return jnp.where(live[None, :, None], scored, jnp.zeros_like(scored))  2.14 us

profile of v2, /device:TPU:0, one launch (start us, length us, event | category | flops | bytes accessed | tf_op | source)
XLA Modules:
  0.0 76.7 jit_solution(13448658843727112730)
XLA Ops:
  1.3 73.2 %score_fused.1 = bf16[1,384,1024]{2,1,0:T(8,128)(2,1)} custom-call(s32[1]{0:T(128)S(6)} %copy.8.length_ref, bf16[1,1024,128]{2,1,0:T(8,128)(2,1)} %hist_ref.1, bf16[1024,512]{1,0:T(8,128)(2,1)} %w_ref.1, bf16[1024,128]{1,0:T(8,128)(2,1)} %wo_ref.1, bf16[1,384,1024]{2,1,0:T(8,128)(2,1)} %cand_ref.1, f32[1,1024]{1,0:T(1,128)} %bitcast.2), custom_call_target="tpu_custom_call" | custom-call | tf_op jit(solution)/shard_map/score_fused/pallas_call | solution.py:311
  74.5 2.1 %broadcast_select_fusion = bf16[1,384,1024]{2,1,0:T(8,128)(2,1)} fusion(bf16[1,384,1024]{2,1,0:T(8,128)(2,1)} %score_fused.1, pred[384]{0:T(512)(128)(4,1)S(1)} %iota_compare_fusion), kind=kLoop, calls=%fused_computation | loop fusion | flops 393216 | bytes 1573248 | tf_op jit(solution)/shard_map/jit(_where)/select_n | solution.py:338
  (1 shorter events, 0.0 us)

commit v3 on v2

--- a/solution.py
+++ b/solution.py
@@ -191,7 +191,7 @@
         side_wait(DIAG, step)
 
     chunk = 128
-    block = 512
+    block = 1024
     length = length_ref[0]
 
     def project_hist(shard):
@@ -213,7 +213,7 @@
     half_scale = 0.5 / math.sqrt(DH)
 
     def attend(first):
-        @pl.loop(0, HEADS // 2)
+        @pl.loop(0, HEADS // 2, unroll=2)
         def _(i):
             head = first + i
             query = pb[2 * HEADS + head]

time: 77 us -> 75.7 us (0.983)
  Pallas kernels: 73.2 us -> 72 us
    pallas_call x1, Pallas kernels: 73.2 us -> 72 us  [fused_shards(): pl.pallas_call(fused_kernel, out_shape=jax.ShapeDtypeStruct(cand_emb.shap...]
where the time goes in v3:
time: 75.7 us; the launch traced here: 75.4 us
  Pallas kernels  72 us (95%)
  other arithmetic  2.15 us (3%)
  between operations  1.31 us (2%)
    pallas_call x1, Pallas kernels, fused_shards(): pl.pallas_call(fused_kernel, out_shape=jax.ShapeDtypeStruct(cand_emb.shap...  72 us
    select_n x1, other arithmetic, fused_shards(): return jnp.where(live[None, :, None], scored, jnp.zeros_like(scored))  2.14 us

profile of v3, /device:TPU:0, one launch (start us, length us, event | category | flops | bytes accessed | tf_op | source)
XLA Modules:
  0.0 75.4 jit_solution(8857565596126420011)
XLA Ops:
  1.3 72.0 %score_fused.1 = bf16[1,384,1024]{2,1,0:T(8,128)(2,1)} custom-call(s32[1]{0:T(128)S(6)} %copy.8.length_ref, bf16[1,1024,128]{2,1,0:T(8,128)(2,1)} %hist_ref.1, bf16[1024,512]{1,0:T(8,128)(2,1)} %w_ref.1, bf16[1024,128]{1,0:T(8,128)(2,1)} %wo_ref.1, bf16[1,384,1024]{2,1,0:T(8,128)(2,1)} %cand_ref.1, f32[1,1024]{1,0:T(1,128)} %bitcast.2), custom_call_target="tpu_custom_call" | custom-call | tf_op jit(solution)/shard_map/score_fused/pallas_call | solution.py:311
  73.3 2.1 %broadcast_select_fusion = bf16[1,384,1024]{2,1,0:T(8,128)(2,1)} fusion(bf16[1,384,1024]{2,1,0:T(8,128)(2,1)} %score_fused.1, pred[384]{0:T(512)(128)(4,1)S(1)} %iota_compare_fusion), kind=kLoop, calls=%fused_computation | loop fusion | flops 393216 | bytes 1573248 | tf_op jit(solution)/shard_map/jit(_where)/select_n | solution.py:338
  (1 shorter events, 0.0 us)

commit v4 on v3

--- a/solution.py
+++ b/solution.py
@@ -213,7 +213,7 @@
     half_scale = 0.5 / math.sqrt(DH)
 
     def attend(first):
-        @pl.loop(0, HEADS // 2, unroll=2)
+        @pl.loop(0, HEADS // 2, unroll=4)
         def _(i):
             head = first + i
             query = pb[2 * HEADS + head]

time: 75.7 us -> 75.3 us (level)
  no operation moved by 1% of the time
where the time goes in v4:
time: 75.3 us; the launch traced here: 75.1 us
  Pallas kernels  71.7 us (95%)
  other arithmetic  2.15 us (3%)
  between operations  1.31 us (2%)
    pallas_call x1, Pallas kernels, fused_shards(): pl.pallas_call(fused_kernel, out_shape=jax.ShapeDtypeStruct(cand_emb.shap...  71.7 us
    select_n x1, other arithmetic, fused_shards(): return jnp.where(live[None, :, None], scored, jnp.zeros_like(scored))  2.14 us

profile of v4, /device:TPU:0, one launch (start us, length us, event | category | flops | bytes accessed | tf_op | source)
XLA Modules:
  0.0 75.1 jit_solution(74679753257883059)
XLA Ops:
  1.3 71.7 %score_fused.1 = bf16[1,384,1024]{2,1,0:T(8,128)(2,1)} custom-call(s32[1]{0:T(128)S(6)} %copy.8.length_ref, bf16[1,1024,128]{2,1,0:T(8,128)(2,1)} %hist_ref.1, bf16[1024,512]{1,0:T(8,128)(2,1)} %w_ref.1, bf16[1024,128]{1,0:T(8,128)(2,1)} %wo_ref.1, bf16[1,384,1024]{2,1,0:T(8,128)(2,1)} %cand_ref.1, f32[1,1024]{1,0:T(1,128)} %bitcast.2), custom_call_target="tpu_custom_call" | custom-call | tf_op jit(solution)/shard_map/score_fused/pallas_call | solution.py:311
  73.0 2.1 %broadcast_select_fusion = bf16[1,384,1024]{2,1,0:T(8,128)(2,1)} fusion(bf16[1,384,1024]{2,1,0:T(8,128)(2,1)} %score_fused.1, pred[384]{0:T(512)(128)(4,1)S(1)} %iota_compare_fusion), kind=kLoop, calls=%fused_computation | loop fusion | flops 393216 | bytes 1573248 | tf_op jit(solution)/shard_map/jit(_where)/select_n | solution.py:338
  (1 shorter events, 0.0 us)
